TPU v7x, 128 devices: a whole 4x4x4 slice. The times are simulated.
128 devices in a mesh: ctx: 64 (over z_lo, x, y, core), fsdp: 2 (over z_hi).
Axes of the slice: x: 4, y: 4, z: 4 (z_hi: 2, z_lo: 2; z = z_hi * 2 + z_lo), core: 2. Of those that a mesh axis runs over, the one named last changes fastest.
Arguments:
- block_in: bfloat16 [2, 8192, 768], P('fsdp', 'ctx'), may hold values from -70 to 70
- out_grad: bfloat16 [2, 8192, 768], P('fsdp', 'ctx'), may hold values from -6 to 6
- ln1_gain: bfloat16 [768], P('fsdp'), may hold values from 0.5 to 1.5
- ln1_bias: bfloat16 [768], P('fsdp'), may hold values from -3 to 3
- w_qkv: bfloat16 [768, 2304], P('fsdp'), may hold values from -2 to 2
- q_bias: bfloat16 [768], P('fsdp'), may hold values from -3 to 3
- v_bias: bfloat16 [768], P('fsdp'), may hold values from -3 to 3
- w_proj: bfloat16 [768, 768], P('fsdp'), may hold values from -2 to 2
- b_proj: bfloat16 [768], P('fsdp'), may hold values from -3 to 3
- ln2_gain: bfloat16 [768], P('fsdp'), may hold values from 0.5 to 1.5
- ln2_bias: bfloat16 [768], P('fsdp'), may hold values from -3 to 3
- w_fc: bfloat16 [768, 3072], P('fsdp'), may hold values from -0.21875 to 0.21875
- b_fc: bfloat16 [3072], P('fsdp'), may hold values from -3 to 3
- w_out: bfloat16 [3072, 768], P('fsdp'), may hold values from -0.109375 to 0.109375
- b_out: bfloat16 [768], P('fsdp'), may hold values from -3 to 3
Outputs:
- block_out: bfloat16 [2, 8192, 768], P('fsdp', 'ctx')
- input_grad: float32 [2, 8192, 768], P('fsdp', 'ctx')
- grad_ln1_gain: float32 [768], P('fsdp')
- grad_ln1_bias: float32 [768], P('fsdp')
- grad_w_qkv: float32 [768, 2304], P('fsdp')
- grad_q_bias: float32 [768], P('fsdp')
- grad_v_bias: float32 [768], P('fsdp')
- grad_w_proj: float32 [768, 768], P('fsdp')
- grad_b_proj: float32 [768], P('fsdp')
- grad_ln2_gain: float32 [768], P('fsdp')
- grad_ln2_bias: float32 [768], P('fsdp')
- grad_w_fc: float32 [768, 3072], P('fsdp')
- grad_b_fc: float32 [3072], P('fsdp')
- grad_w_out: float32 [3072, 768], P('fsdp')
- grad_b_out: float32 [768], P('fsdp')
All inputs are finite; a program needn't handle non-finite values.
Results may differ from a plain program's by a relative error of at most 0.025.
The roundings to bfloat16 on the way count: a program that leaves them out, or rounds other values in their place, can miss the bound.
Values may be sent and summed in bfloat16 or wider, within the bound.
No kernel may reach another device: no remote copies, remote signals or barrier semaphores. Data moves between devices by JAX's collectives and lax.ppermute only.
A program may use at most 256 MiB of HBM per device.

v0:
```python
import math
import jax
import jax.numpy as jnp
from jax import lax
from jax.sharding import PartitionSpec as P

HEADS = 12
norm_epsilon = 1e-05
gelu_factor = 0.7978845608028654
gelu_cubic = 0.044715
masked_score = -1e30


def layer_norm(values, gain, offset):
    center = jnp.mean(values, axis=-1, keepdims=True)
    centered = values - center
    spread = jnp.mean(centered * centered, axis=-1, keepdims=True)
    return centered * lax.rsqrt(spread + norm_epsilon) * gain + offset


def gelu_tanh(values):
    return (
        0.5
        * values
        * (1.0 + jnp.tanh(gelu_factor * (values + gelu_cubic * values * values * values)))
    )


def score_grads(
    query_rows, grad_rows, lse_rows, delta_rows, key_rows, value_rows, allowed, score_scale
):
    scores = (
        jnp.einsum("thd,shd->hts", query_rows, key_rows, preferred_element_type=jnp.float32)
        * score_scale
    )
    scores = jnp.where(allowed[None], scores, masked_score)
    probabilities = jnp.where(allowed[None], jnp.exp(scores - lse_rows[:, :, None]), 0.0)
    grad_probs = jnp.einsum(
        "thd,shd->hts", grad_rows, value_rows, preferred_element_type=jnp.float32
    )
    grad_scores = (probabilities * (grad_probs - delta_rows[:, :, None]) * score_scale).astype(
        jnp.bfloat16
    )
    return (grad_scores, probabilities)


def body(
    block_in,
    out_grad,
    ln1_gain,
    ln1_bias,
    w_qkv,
    q_bias,
    v_bias,
    w_proj,
    b_proj,
    ln2_gain,
    ln2_bias,
    w_fc,
    b_fc,
    w_out,
    b_out,
):
    gathered = (
        lax.all_gather(ln1_gain, "fsdp", axis=0, tiled=True),
        lax.all_gather(ln1_bias, "fsdp", axis=0, tiled=True),
        lax.all_gather(w_qkv, "fsdp", axis=0, tiled=True),
        lax.all_gather(q_bias, "fsdp", axis=0, tiled=True),
        lax.all_gather(v_bias, "fsdp", axis=0, tiled=True),
        lax.all_gather(w_proj, "fsdp", axis=0, tiled=True),
        lax.all_gather(b_proj, "fsdp", axis=0, tiled=True),
        lax.all_gather(ln2_gain, "fsdp", axis=0, tiled=True),
        lax.all_gather(ln2_bias, "fsdp", axis=0, tiled=True),
        lax.all_gather(w_fc, "fsdp", axis=0, tiled=True),
        lax.all_gather(b_fc, "fsdp", axis=0, tiled=True),
        lax.all_gather(w_out, "fsdp", axis=0, tiled=True),
        lax.all_gather(b_out, "fsdp", axis=0, tiled=True),
    )
    gain_one = gathered[0].astype(jnp.float32)
    shift_one = gathered[1].astype(jnp.float32)
    qkv_weight = gathered[2]
    query_bias = gathered[3].astype(jnp.float32)
    value_bias = gathered[4].astype(jnp.float32)
    proj_weight = gathered[5]
    proj_bias = gathered[6].astype(jnp.float32)
    gain_two = gathered[7].astype(jnp.float32)
    shift_two = gathered[8].astype(jnp.float32)
    fc_weight = gathered[9]
    fc_bias = gathered[10].astype(jnp.float32)
    out_weight = gathered[11]
    out_bias = gathered[12].astype(jnp.float32)
    row_count = block_in.shape[1]
    width = block_in.shape[2]
    head_count = HEADS
    head_width = width // head_count
    score_scale = 1.0 / math.sqrt(head_width)
    row_total = row_count * lax.axis_size("ctx")
    first_query = lax.axis_index("ctx") * row_count
    query_pos = first_query + jnp.arange(row_count, dtype=jnp.int32)
    last_query = first_query + row_count - 1
    inputs_wide = block_in[0].astype(jnp.float32)
    normed_one = layer_norm(inputs_wide, gain_one, shift_one).astype(jnp.bfloat16)
    projected = jnp.dot(normed_one, qkv_weight, preferred_element_type=jnp.float32)
    queries = (projected[:, :width] + query_bias).astype(jnp.bfloat16)
    keys_local = projected[:, width : 2 * width].astype(jnp.bfloat16)
    values_local = (projected[:, 2 * width :] + value_bias).astype(jnp.bfloat16)
    query_heads = queries.reshape(row_count, head_count, head_width)
    initial = (
        jnp.full((head_count, row_count), masked_score, jnp.float32),
        jnp.zeros((head_count, row_count), jnp.float32),
        jnp.zeros((row_count, head_count, head_width), jnp.float32),
    )
    key_span = lax.all_gather(keys_local, "ctx", axis=0, tiled=True)
    value_span = lax.all_gather(values_local, "ctx", axis=0, tiled=True)
    span_total = key_span.shape[0]
    attend_span_rows = math.gcd(span_total, 512)

    def one_step(step_index, inner):
        offset = step_index * attend_span_rows
        key_rows = lax.dynamic_slice_in_dim(key_span, offset, attend_span_rows, 0).reshape(
            attend_span_rows, head_count, head_width
        )
        value_rows = lax.dynamic_slice_in_dim(value_span, offset, attend_span_rows, 0).reshape(
            attend_span_rows, head_count, head_width
        )

        def one_computed(state):
            maximum, denominator, accumulated = state
            key_pos = offset + jnp.arange(attend_span_rows, dtype=jnp.int32)
            allowed = key_pos[None, :] <= query_pos[:, None]
            scores = (
                jnp.einsum(
                    "thd,shd->hts", query_heads, key_rows, preferred_element_type=jnp.float32
                )
                * score_scale
            )
            scores = jnp.where(allowed[None], scores, masked_score)
            new_max = jnp.maximum(maximum, jnp.max(scores, axis=2))
            weights = jnp.where(allowed[None], jnp.exp(scores - new_max[:, :, None]), 0.0)
            factor = jnp.exp(maximum - new_max)
            denominator = denominator * factor + jnp.sum(weights, axis=2)
            accumulated = accumulated * jnp.transpose(factor)[:, :, None] + jnp.einsum(
                "hts,shd->thd",
                weights.astype(jnp.bfloat16),
                value_rows,
                preferred_element_type=jnp.float32,
            )
            return (new_max, denominator, accumulated)

        return lax.cond(offset > last_query, lambda state: state, one_computed, inner)

    maximum, denominator, accumulated = lax.fori_loop(
        0, span_total // attend_span_rows, one_step, initial
    )
    log_sums = maximum + jnp.log(denominator)
    attended = accumulated / jnp.transpose(denominator)[:, :, None]
    attn_rows = lax.optimization_barrier(attended.reshape(row_count, width).astype(jnp.bfloat16))
    residual_one = (
        jnp.dot(attn_rows, proj_weight, preferred_element_type=jnp.float32)
        + proj_bias
        + inputs_wide
    )
    normed_two = layer_norm(residual_one, gain_two, shift_two).astype(jnp.bfloat16)
    hidden_pre = jnp.dot(normed_two, fc_weight, preferred_element_type=jnp.float32) + fc_bias
    activated = gelu_tanh(hidden_pre).astype(jnp.bfloat16)
    output = (
        jnp.dot(activated, out_weight, preferred_element_type=jnp.float32) + out_bias + residual_one
    ).astype(jnp.bfloat16)
    cotangent = out_grad[0]
    grad_wide = cotangent.astype(jnp.float32)
    grad_out_weight = jnp.einsum(
        "tf,td->fd", activated, cotangent, preferred_element_type=jnp.float32
    )
    grad_out_bias = jnp.sum(grad_wide, axis=0)
    grad_activated = jnp.einsum(
        "td,fd->tf", cotangent, out_weight, preferred_element_type=jnp.float32
    )
    unused, gelu_back = jax.vjp(gelu_tanh, hidden_pre)
    grad_hidden = gelu_back(grad_activated)[0]
    grad_hidden_low = grad_hidden.astype(jnp.bfloat16)
    grad_fc_weight = jnp.einsum(
        "td,tf->df", normed_two, grad_hidden_low, preferred_element_type=jnp.float32
    )
    grad_fc_bias = jnp.sum(grad_hidden, axis=0)
    grad_normed_two = jnp.einsum(
        "tf,df->td", grad_hidden_low, fc_weight, preferred_element_type=jnp.float32
    )
    unused, norm_back_two = jax.vjp(layer_norm, residual_one, gain_two, shift_two)
    grad_residual, grad_gain_two, grad_shift_two = norm_back_two(grad_normed_two)
    grad_residual = grad_residual + grad_wide
    grad_residual_low = grad_residual.astype(jnp.bfloat16)
    grad_proj_weight = jnp.einsum(
        "td,te->de", attn_rows, grad_residual_low, preferred_element_type=jnp.float32
    )
    grad_proj_bias = jnp.sum(grad_residual, axis=0)
    grad_attn = lax.optimization_barrier(
        jnp.einsum(
            "te,de->td", grad_residual_low, proj_weight, preferred_element_type=jnp.float32
        ).astype(jnp.bfloat16)
    )
    grad_heads = grad_attn.reshape(row_count, head_count, head_width)
    delta_sums = jnp.transpose(
        jnp.sum(
            grad_heads.astype(jnp.float32)
            * attn_rows.reshape(row_count, head_count, head_width).astype(jnp.float32),
            axis=2,
        )
    )
    keys_all, values_all = (
        lax.all_gather(keys_local, "ctx", axis=0, tiled=True),
        lax.all_gather(values_local, "ctx", axis=0, tiled=True),
    )
    span_rows = math.gcd(row_total, 512)
    span_count = row_total // span_rows
    key_blocks = keys_all.reshape(span_count, span_rows, head_count, head_width)
    value_blocks = values_all.reshape(span_count, span_rows, head_count, head_width)
    zero_query = jnp.zeros((row_count, head_count, head_width), jnp.float32)

    def back_step(grad_query, inputs):
        key_rows, value_rows, step_index = inputs
        start_pos = step_index * span_rows

        def back_computed(running):
            key_pos = start_pos + jnp.arange(span_rows, dtype=jnp.int32)
            allowed = key_pos[None, :] <= query_pos[:, None]
            grad_scores, probabilities = score_grads(
                query_heads,
                grad_heads,
                log_sums,
                delta_sums,
                key_rows,
                value_rows,
                allowed,
                score_scale,
            )
            rounded = probabilities.astype(jnp.bfloat16)
            grad_key = jnp.einsum(
                "hts,thd->shd", grad_scores, query_heads, preferred_element_type=jnp.float32
            )
            grad_value = jnp.einsum(
                "hts,thd->shd", rounded, grad_heads, preferred_element_type=jnp.float32
            )
            updated = running + jnp.einsum(
                "hts,shd->thd", grad_scores, key_rows, preferred_element_type=jnp.float32
            )
            return (
                updated,
                jnp.concatenate(
                    [grad_key.reshape(span_rows, width), grad_value.reshape(span_rows, width)],
                    axis=1,
                ),
            )

        def skipped(running):
            return (running, jnp.zeros((span_rows, 2 * width), jnp.float32))

        return lax.cond(start_pos > last_query, skipped, back_computed, grad_query)

    grad_query, key_terms = lax.scan(
        back_step, zero_query, (key_blocks, value_blocks, jnp.arange(span_count, dtype=jnp.int32))
    )
    own_terms = lax.psum_scatter(
        key_terms.reshape(row_total, 2 * width), "ctx", scatter_dimension=0, tiled=True
    )
    grad_keys = own_terms[:, :width]
    grad_values = own_terms[:, width:]
    grad_query = grad_query.reshape(row_count, width)
    grad_query_bias = jnp.sum(grad_query, axis=0)
    grad_value_bias = jnp.sum(grad_values, axis=0)
    grad_projected = jnp.concatenate([grad_query, grad_keys, grad_values], axis=1).astype(
        jnp.bfloat16
    )
    grad_qkv_weight = jnp.einsum(
        "td,te->de", normed_one, grad_projected, preferred_element_type=jnp.float32
    )
    grad_normed_one = jnp.einsum(
        "te,de->td", grad_projected, qkv_weight, preferred_element_type=jnp.float32
    )
    unused, norm_back_one = jax.vjp(layer_norm, inputs_wide, gain_one, shift_one)
    grad_inputs, grad_gain_one, grad_shift_one = norm_back_one(grad_normed_one)
    grad_inputs = grad_inputs + grad_residual
    shards = (
        lax.psum_scatter(
            grad_gain_one.astype(jnp.bfloat16), "fsdp", scatter_dimension=0, tiled=True
        ).astype(jnp.float32),
        lax.psum_scatter(
            grad_shift_one.astype(jnp.bfloat16), "fsdp", scatter_dimension=0, tiled=True
        ).astype(jnp.float32),
        lax.psum_scatter(
            grad_qkv_weight.astype(jnp.bfloat16), "fsdp", scatter_dimension=0, tiled=True
        ).astype(jnp.float32),
        lax.psum_scatter(
            grad_query_bias.astype(jnp.bfloat16), "fsdp", scatter_dimension=0, tiled=True
        ).astype(jnp.float32),
        lax.psum_scatter(
            grad_value_bias.astype(jnp.bfloat16), "fsdp", scatter_dimension=0, tiled=True
        ).astype(jnp.float32),
        lax.psum_scatter(
            grad_proj_weight.astype(jnp.bfloat16), "fsdp", scatter_dimension=0, tiled=True
        ).astype(jnp.float32),
        lax.psum_scatter(
            grad_proj_bias.astype(jnp.bfloat16), "fsdp", scatter_dimension=0, tiled=True
        ).astype(jnp.float32),
        lax.psum_scatter(
            grad_gain_two.astype(jnp.bfloat16), "fsdp", scatter_dimension=0, tiled=True
        ).astype(jnp.float32),
        lax.psum_scatter(
            grad_shift_two.astype(jnp.bfloat16), "fsdp", scatter_dimension=0, tiled=True
        ).astype(jnp.float32),
        lax.psum_scatter(
            grad_fc_weight.astype(jnp.bfloat16), "fsdp", scatter_dimension=0, tiled=True
        ).astype(jnp.float32),
        lax.psum_scatter(
            grad_fc_bias.astype(jnp.bfloat16), "fsdp", scatter_dimension=0, tiled=True
        ).astype(jnp.float32),
        lax.psum_scatter(
            grad_out_weight.astype(jnp.bfloat16), "fsdp", scatter_dimension=0, tiled=True
        ).astype(jnp.float32),
        lax.psum_scatter(
            grad_out_bias.astype(jnp.bfloat16), "fsdp", scatter_dimension=0, tiled=True
        ).astype(jnp.float32),
    )
    totals = lax.psum(
        (
            shards[0],
            shards[1],
            shards[2],
            shards[3],
            shards[4],
            shards[5],
            shards[6],
            shards[7],
            shards[8],
            shards[9],
            shards[10],
            shards[11],
            shards[12],
        ),
        "ctx",
    )
    return (
        output[None],
        grad_inputs[None],
        totals[0],
        totals[1],
        totals[2],
        totals[3],
        totals[4],
        totals[5],
        totals[6],
        totals[7],
        totals[8],
        totals[9],
        totals[10],
        totals[11],
        totals[12],
    )


def solution(mesh):
    in_specs = (
        P("fsdp", "ctx", None),
        P("fsdp", "ctx", None),
        P("fsdp"),
        P("fsdp"),
        P("fsdp", None),
        P("fsdp"),
        P("fsdp"),
        P("fsdp", None),
        P("fsdp"),
        P("fsdp"),
        P("fsdp"),
        P("fsdp", None),
        P("fsdp"),
        P("fsdp", None),
        P("fsdp"),
    )
    out_specs = (
        P("fsdp", "ctx", None),
        P("fsdp", "ctx", None),
        P("fsdp"),
        P("fsdp"),
        P("fsdp", None),
        P("fsdp"),
        P("fsdp"),
        P("fsdp", None),
        P("fsdp"),
        P("fsdp"),
        P("fsdp"),
        P("fsdp", None),
        P("fsdp"),
        P("fsdp", None),
        P("fsdp"),
    )
    return jax.shard_map(body, mesh=mesh, in_specs=in_specs, out_specs=out_specs, check_vma=False)
```

profile of v0, /device:TPU:0, one launch (start us, length us, event | category | flops | bytes accessed | tf_op | source)
XLA Modules:
  0.0 1733.6 jit_solution(4564429500221950973)
XLA Ops:
  8.7 6.2 all-gather.1
  24.4 41.3 %all-gather.16.cloned.1.call-done = bf16[768,2304]{1,0:T(8,128)(2,1)} async-done(((bf16[384,2304]{1,0:T(8,128)(2,1)}), bf16[768,2304]{1,0:T(8,128)(2,1)}) %all-gather.16.cloned.1.call-update) | async-done | bytes 3538960 | tf_op jit(solution)/shard_map/all_gather | solution.py:67
  83.8 5.8 all-gather.4
  89.7 5.9 all-gather.7
  95.6 5.8 all-gather.6
  107.5 79.1 %all-gather.18.cloned.1.call-done = bf16[8192,768]{1,0:T(8,128)(2,1)} async-done(((bf16[128,768]{1,0:T(8,128)(2,1)}), bf16[8192,768]{1,0:T(8,128)(2,1)}) %all-gather.18.cloned.1.call-update) | async-done | bytes 12582928 | tf_op jit(solution)/shard_map/all_gather | solution.py:113
  186.6 16.3 copy.76
  203.0 103.3 %all-gather.20.cloned.1.call-done = bf16[8192,768]{1,0:T(8,128)(2,1)} async-done(((bf16[128,768]{1,0:T(8,128)(2,1)}), bf16[8192,768]{1,0:T(8,128)(2,1)}) %all-gather.20.cloned.1.call-update) | async-done | bytes 12582928 | tf_op jit(solution)/shard_map/all_gather | solution.py:114
  306.2 15.8 copy.77
  327.9 6.2 all-gather.22.cloned.1.call-done
  336.0 65.6 %all-gather.24.cloned.1.call-done = bf16[768,3072]{1,0:T(8,128)(2,1)} async-done(((bf16[384,3072]{1,0:T(8,128)(2,1)}), bf16[768,3072]{1,0:T(8,128)(2,1)}) %all-gather.24.cloned.1.call-update) | async-done | bytes 4718608 | tf_op jit(solution)/shard_map/all_gather | solution.py:74
  404.9 64.3 %all-gather.26.cloned.1.call-done = bf16[3072,768]{1,0:T(8,128)(2,1)} async-done(((bf16[1536,768]{1,0:T(8,128)(2,1)}), bf16[3072,768]{1,0:T(8,128)(2,1)}) %all-gather.26.cloned.1.call-update) | async-done | bytes 4718608 | tf_op jit(solution)/shard_map/all_gather | solution.py:76
  477.3 9.5 copy.108
  486.9 18.8 %copy.81 = bf16[16,512,12,64]{1,3,2,0:T(8,128)(2,1)} copy(bf16[16,512,12,64]{1,0,3,2:T(8,128)(2,1)S(1)} %bitcast.175) | data formatting | bytes 25165824
  510.9 18.6 %copy.82 = bf16[16,512,12,64]{1,3,2,0:T(8,128)(2,1)} copy(bf16[16,512,12,64]{1,0,3,2:T(8,128)(2,1)S(1)} %bitcast.176) | data formatting | bytes 25165824
  532.7 134.6 %while.35 = (s32[]{:T(128)}, f32[128,12,64]{0,2,1:T(8,128)}, f32[16,512,1536]{2,1,0:T(8,128)}, s32[16]{0:T(128)S(1)}, s32[]{:T(128)}, /*index=5*/bf16[16,512,12,...) while((s32[]{:T(128)}, f32[128,12,64]{0,2,1:T(8,128)}, ...), condition=%wide.region_16.17_spmd.clone, body=%wide.region_13.16_spmd.clone.sunk | while | flops 514491008 | bytes 40333600 | solution.py:259
  533.9 10.1 conditional.7
  680.5 502.5 %reduce-scatter.6.cloned.1.call-done = f32[128,1536]{1,0:T(8,128)} async-done(((f32[8192,1536]{1,0:T(8,128)}), f32[128,1536]{1,0:T(8,128)}) %reduce-scatter.6.cloned.1.call-update) | async-done | bytes 786448 | tf_op jit(solution)/shard_map/reduce_scatter | solution.py:262
  1202.3 7.9 reduce-scatter.10.cloned.1.call-done
  1210.2 66.5 %reduce-scatter.12.cloned.1.call-done = bf16[384,3072]{1,0:T(8,128)(2,1)} async-done(((bf16[768,3072]{1,0:T(8,128)(2,1)}), bf16[384,3072]{1,0:T(8,128)(2,1)}) %reduce-scatter.12.cloned.1.call-update) | async-done | bytes 2359312 | tf_op jit(solution)/shard_map/reduce_scatter | solution.py:310
  1276.7 66.2 %reduce-scatter.14.cloned.1.call-done = bf16[1536,768]{1,0:T(8,128)(2,1)} async-done(((bf16[3072,768]{1,0:T(8,128)(2,1)}), bf16[1536,768]{1,0:T(8,128)(2,1)}) %reduce-scatter.14.cloned.1.call-update) | async-done | bytes 2359312 | tf_op jit(solution)/shard_map/reduce_scatter | solution.py:316
  1348.1 8.4 all-reduce.10
  1356.9 40.2 %reduce-scatter.8.cloned.1.call-done = bf16[384,2304]{1,0:T(8,128)(2,1)} async-done(((bf16[768,2304]{1,0:T(8,128)(2,1)}), bf16[384,2304]{1,0:T(8,128)(2,1)}) %reduce-scatter.8.cloned.1.call-update) | async-done | bytes 1769488 | tf_op jit(solution)/shard_map/reduce_scatter | solution.py:289
  1397.1 330.0 %all-reduce.12 = (f32[384]{0:T(512)}, f32[384]{0:T(512)}, f32[384,2304]{1,0:T(8,128)}, f32[384]{0:T(512)}, f32[384]{0:T(512)}, /*index=5*/f32[384,768]{1,0:T(8,1...) all-reduce(f32[384]{0:T(512)S(1)} %get-tuple-element.680, ...), channel_id=1, replica_groups=mesh['ctx'=64,'fsdp'=2] {'ctx'}, use_global_device_ids=true, to_apply=%region_22.23 | all-reduce | flops 3543552 | bytes 21270528 | tf_op jit(solution)/shard_map/psum | solution.py:323
  (404 shorter events, 237.4 us)
Async XLA Ops:
  7.2 58.5 %all-gather.16.cloned.1.call-start = ((), (), s32[]{:S(2)}) async-start(), calls=%async_computation.5 | async-start | bytes 5308416 | tf_op jit(solution)/shard_map/all_gather | solution.py:67
  7.9 178.7 %all-gather.18.cloned.1.call-start = ((), (), s32[]{:S(2)}) async-start(), calls=%async_computation.6 | async-start | bytes 12779520 | tf_op jit(solution)/shard_map/all_gather | solution.py:113
  69.3 237.0 %all-gather.20.cloned.1.call-start = ((), (), s32[]{:S(2)}) async-start(), calls=%async_computation.7 | async-start | bytes 12779520 | tf_op jit(solution)/shard_map/all_gather | solution.py:114
  81.9 252.1 %all-gather.22.cloned.1.call-start = ((), (), s32[]{:S(2)}) async-start(), calls=%async_computation.8 | async-start | bytes 1769472 | tf_op jit(solution)/shard_map/all_gather | solution.py:70
  82.5 319.1 %all-gather.24.cloned.1.call-start = ((), (), s32[]{:S(2)}) async-start(), calls=%async_computation.9 | async-start | bytes 7077888 | tf_op jit(solution)/shard_map/all_gather | solution.py:74
  83.1 386.1 %all-gather.26.cloned.1.call-start = ((), (), s32[]{:S(2)}) async-start(), calls=%async_computation.10 | async-start | bytes 7077888 | tf_op jit(solution)/shard_map/all_gather | solution.py:76
  83.7 1099.3 %reduce-scatter.6.cloned.1.call-start = ((), (), s32[]{:S(2)}) async-start(), calls=%async_computation.11 | async-start | bytes 51118080 | tf_op jit(solution)/shard_map/reduce_scatter | solution.py:262
  101.5 300.2 %copy-start.24 = (f32[768]{0:T(1024)}, f32[768]{0:T(1024)S(1)}, u32[]{:S(2)}) copy-start(f32[768]{0:T(1024)S(1)} %reshape.258) | copy-start | bytes 9220
  107.4 294.3 %copy-start.21 = (f32[768]{0:T(1024)}, f32[768]{0:T(1024)S(1)}, u32[]{:S(2)}) copy-start(f32[768]{0:T(1024)S(1)} %reshape.257) | copy-start | bytes 9220
  327.9 202.9 %copy-start.11 = (bf16[128,12,64]{0,2,1:T(8,128)(2,1)}, bf16[128,12,64]{0,2,1:T(8,128)(2,1)S(1)}, u32[]{:S(2)}) copy-start(bf16[128,12,64]{0,2,1:T(8,128)(2,1)S(1)} %divide_convert_fusion) | copy-start | bytes 589828
  335.8 141.2 %copy-start.1 = (f32[128,768]{1,0:T(8,128)}, f32[128,768]{1,0:T(8,128)S(1)}, u32[]{:S(2)}) copy-start(f32[128,768]{1,0:T(8,128)S(1)} %get-tuple-element.668) | copy-start | bytes 1179652
  404.9 69.7 %copy-start.3 = (f32[128,3072]{1,0:T(8,128)}, f32[128,3072]{1,0:T(8,128)S(1)}, u32[]{:S(2)}) copy-start(f32[128,3072]{1,0:T(8,128)S(1)} %convolution_add_fusion) | copy-start | bytes 4718596
  667.3 542.8 %reduce-scatter.10.cloned.1.call-start = ((), (), s32[]{:S(2)}) async-start(), calls=%async_computation.13 | async-start | bytes 1769472 | tf_op jit(solution)/shard_map/reduce_scatter | solution.py:298
  669.9 606.8 %reduce-scatter.12.cloned.1.call-start = ((), (), s32[]{:S(2)}) async-start(), calls=%async_computation.14 | async-start | bytes 7077888 | tf_op jit(solution)/shard_map/reduce_scatter | solution.py:310
  673.8 669.2 %reduce-scatter.14.cloned.1.call-start = ((), (), s32[]{:S(2)}) async-start(), calls=%async_computation.15 | async-start | bytes 7077888 | tf_op jit(solution)/shard_map/reduce_scatter | solution.py:316
  679.0 505.2 %copy-start.20 = (f32[768]{0:T(1024)S(1)}, f32[768]{0:T(1024)}, u32[]{:S(2)}) copy-start(f32[768]{0:T(1024)} %copy-done.19) | copy-start | bytes 9220
  679.0 505.2 %copy-start.27 = (f32[768]{0:T(1024)S(1)}, f32[768]{0:T(1024)}, u32[]{:S(2)}) copy-start(f32[768]{0:T(1024)} %copy-done.26) | copy-start | bytes 9220
  679.0 505.2 %copy-start.32 = (f32[128]{0:T(128)S(1)}, f32[128]{0:T(128)}, u32[]{:S(2)}) copy-start(f32[128]{0:T(128)} %copy-done.31) | copy-start | bytes 1540
  679.0 718.1 %reduce-scatter.8.cloned.1.call-start = ((), (), s32[]{:S(2)}) async-start(), calls=%async_computation.12 | async-start | bytes 5308416 | tf_op jit(solution)/shard_map/reduce_scatter | solution.py:289
  680.5 507.3 %copy-start.17 = (bf16[128,768]{1,0:T(8,128)(2,1)}, bf16[128,768]{1,0:T(8,128)(2,1)S(1)}, u32[]{:S(2)}) copy-start(bf16[128,768]{1,0:T(8,128)(2,1)S(1)} %copy.84) | copy-start | bytes 589828
  1198.1 144.8 %copy-start.15 = (f32[128,1536]{1,0:T(8,128)S(1)}, f32[128,1536]{1,0:T(8,128)}, u32[]{:S(2)}) copy-start(f32[128,1536]{1,0:T(8,128)} %reduce-scatter.6.cloned.1.call-done) | copy-start | bytes 2359300
  1202.3 144.4 %copy-start.54 = (f32[128]{0:T(128)S(1)}, f32[128]{0:T(128)}, u32[]{:S(2)}) copy-start(f32[128]{0:T(128)} %copy-done.53) | copy-start | bytes 1540
  1202.3 144.5 %copy-start.37 = (f32[128]{0:T(128)S(1)}, f32[128]{0:T(128)}, u32[]{:S(2)}) copy-start(f32[128]{0:T(128)} %copy-done.36) | copy-start | bytes 1540
  1202.3 144.8 %copy-start.45 = (f32[128]{0:T(128)S(1)}, f32[128]{0:T(128)}, u32[]{:S(2)}) copy-start(f32[128]{0:T(128)} %copy-done.43) | copy-start | bytes 1540
  (48 other events, 1023.4 us)
Sparse Core Ops, SparseCore 0:
  9.7 56.0 all-gather.15
  69.4 117.2 all-gather.17
  188.9 117.2 all-gather.19
  307.7 26.2 all-gather.21
  335.6 66.0 all-gather.23
  403.1 66.0 all-gather.25
  667.4 515.5 reduce-scatter.5
  1185.9 24.1 reduce-scatter.9
  1213.3 63.3 reduce-scatter.11
  1279.5 63.3 reduce-scatter.13
  1346.0 51.0 reduce-scatter.7
where the time goes:
time: 1740 us; the launch traced here: 1730 us
  waiting for transfers between devices  1050 us (60%)
  blocking collectives  391 us (22%)
  local copies, waits for them, and re-layouts  208 us (12%)
  matrix products  48 us (3%)
    reduce_scatter x1, waiting for transfers between devices, body(): lax.psum_scatter(key_terms.reshape(row_total, 2 * width), 'ctx', scatter_...  503 us
    psum x1, blocking collectives, body(): lax.psum((shards[0], shards[1], shards[2], shards[3], shards[4], shards[5...  330 us
    all_gather x1, waiting for transfers between devices, body(): value_span = lax.all_gather(values_local, 'ctx', axis=0, tiled=True)  103 us
    dynamic_update_slice x32, local copies, waits for them, and re-layouts, body(): lax.scan(back_step, zero_query, (key_blocks, value_blocks, jnp.arange(spa...  98.1 us
    unnamed x138, local copies, waits for them, and re-layouts  89.2 us
    all_gather x1, waiting for transfers between devices, body(): key_span = lax.all_gather(keys_local, 'ctx', axis=0, tiled=True)  79.1 us
    reduce_scatter x1, waiting for transfers between devices, body(): lax.psum_scatter(grad_fc_weight.astype(jnp.bfloat16), 'fsdp', scatter_dim...  66.5 us
    reduce_scatter x1, waiting for transfers between devices, body(): lax.psum_scatter(grad_out_weight.astype(jnp.bfloat16), 'fsdp', scatter_di...  66.2 us
  transfers between devices with their start and end apart: 11, of which 11 were waited for; matrix products, arithmetic and copies ran while one was open for 4% of the time, Pallas kernels for 0%

commit v1 on v0

--- a/solution.py
+++ b/solution.py
@@ -110,8 +110,13 @@
         jnp.zeros((head_count, row_count), jnp.float32),
         jnp.zeros((row_count, head_count, head_width), jnp.float32),
     )
-    key_span = lax.all_gather(keys_local, "ctx", axis=0, tiled=True)
-    value_span = lax.all_gather(values_local, "ctx", axis=0, tiled=True)
+    key_span, value_span = jnp.split(
+        lax.all_gather(
+            jnp.concatenate([keys_local, values_local], axis=1), "ctx", axis=0, tiled=True
+        ),
+        [keys_local.shape[1]],
+        axis=1,
+    )
     span_total = key_span.shape[0]
     attend_span_rows = math.gcd(span_total, 512)
 

time: 1740 us -> 1830 us (1.052)
  local copies, waits for them, and re-layouts: 208 us -> 262 us
  waiting for transfers between devices: 1050 us -> 1080 us
    all_gather x2 -> x3, waiting for transfers between devices: 182 us -> 253 us  [the longest x1 101 us: body(): lax.all_gather(jnp.concatenate([keys_local, values_local], axis=1), 'ctx'...]
    all_gather x0 -> x2, local copies, waits for them, and re-layouts: none -> 32.4 us  [the longest x1 16.3 us: body(): lax.all_gather(keys_local, 'ctx', axis=0, tiled=True)]
    all_gather x1, waiting for transfers between devices: 65.6 us -> 39.4 us  [body(): lax.all_gather(w_fc, 'fsdp', axis=0, tiled=True)]
    unnamed x138 -> x132, local copies, waits for them, and re-layouts: 89.2 us -> 94 us
  transfers between devices with their start and end apart: 11 -> 12, of which waited for: 11 -> 11; matrix products, arithmetic and copies ran while one was open for 4% -> 10% of each run, Pallas kernels for 0% -> 0%
where the time goes in v1:
time: 1830 us
  waiting for transfers between devices  1080 us (59%)
  blocking collectives  392 us (21%)
  local copies, waits for them, and re-layouts  262 us (14%)
  matrix products  48 us (3%)
    reduce_scatter x1, waiting for transfers between devices, body(): lax.psum_scatter(key_terms.reshape(row_total, 2 * width), 'ctx', scatter_...  502 us
    psum x1, blocking collectives, body(): lax.psum((shards[0], shards[1], shards[2], shards[3], shards[4], shards[5...  330 us
    all_gather x1, waiting for transfers between devices, body(): lax.all_gather(jnp.concatenate([keys_local, values_local], axis=1), 'ctx'...  101 us
    dynamic_update_slice x32, local copies, waits for them, and re-layouts, body(): lax.scan(back_step, zero_query, (key_blocks, value_blocks, jnp.arange(spa...  98 us
    unnamed x132, local copies, waits for them, and re-layouts  94 us
    all_gather x1, waiting for transfers between devices, body(): lax.all_gather(keys_local, 'ctx', axis=0, tiled=True)  77.3 us
    all_gather x1, waiting for transfers between devices, body(): lax.all_gather(values_local, 'ctx', axis=0, tiled=True)  75.2 us
    reduce_scatter x1, waiting for transfers between devices, body(): lax.psum_scatter(grad_out_weight.astype(jnp.bfloat16), 'fsdp', scatter_di...  66.4 us
  transfers between devices with their start and end apart: 12, of which 11 were waited for; matrix products, arithmetic and copies ran while one was open for 10% of the time, Pallas kernels for 0%

profile of v1, /device:TPU:0, one launch (start us, length us, event | category | flops | bytes accessed | tf_op | source)
XLA Modules:
  0.0 1828.3 jit_solution(14699210527768904887)
XLA Ops:
  24.3 41.4 %all-gather.17.cloned.1.call-done = bf16[768,2304]{1,0:T(8,128)(2,1)} async-done(((bf16[384,2304]{1,0:T(8,128)(2,1)}), bf16[768,2304]{1,0:T(8,128)(2,1)}) %all-gather.17.cloned.1.call-update) | async-done | bytes 3538960 | tf_op jit(solution)/shard_map/all_gather | solution.py:67
  109.6 77.3 %all-gather.27.cloned.1.call-done = bf16[8192,768]{1,0:T(8,128)(2,1)} async-done(((bf16[128,768]{1,0:T(8,128)(2,1)}), bf16[8192,768]{1,0:T(8,128)(2,1)}) %all-gather.27.cloned.1.call-update) | async-done | bytes 12582928 | tf_op jit(solution)/shard_map/all_gather | solution.py:215
  186.9 16.3 copy.78
  203.1 9.4 copy.108
  212.6 18.6 %copy.81 = bf16[16,512,12,64]{1,3,2,0:T(8,128)(2,1)} copy(bf16[16,512,12,64]{1,0,3,2:T(8,128)(2,1)S(1)} %bitcast.172) | data formatting | bytes 25165824
  231.1 75.2 %all-gather.29.cloned.1.call-done = bf16[8192,768]{1,0:T(8,128)(2,1)} async-done(((bf16[128,768]{1,0:T(8,128)(2,1)}), bf16[8192,768]{1,0:T(8,128)(2,1)}) %all-gather.29.cloned.1.call-update) | async-done | bytes 12582928 | tf_op jit(solution)/shard_map/all_gather | solution.py:216
  306.3 16.2 copy.79
  322.5 9.6 copy.109
  332.1 18.6 %copy.82 = bf16[16,512,12,64]{1,3,2,0:T(8,128)(2,1)} copy(bf16[16,512,12,64]{1,0,3,2:T(8,128)(2,1)S(1)} %bitcast.174) | data formatting | bytes 25165824
  350.6 101.0 %all-gather.19.cloned.1.call-done = bf16[8192,1536]{1,0:T(8,128)(2,1)} async-done(((bf16[128,1536]{1,0:T(8,128)(2,1)}), bf16[8192,1536]{1,0:T(8,128)(2,1)}) %all-gather.19.cloned.1.call-update) | async-done | bytes 25165840 | tf_op jit(solution)/shard_map/all_gather | solution.py:114
  451.6 17.2 fusion.93
  468.8 15.8 copy.76
  484.6 16.3 copy.77
  509.0 39.4 %all-gather.23.cloned.1.call-done = bf16[768,3072]{1,0:T(8,128)(2,1)} async-done(((bf16[384,3072]{1,0:T(8,128)(2,1)}), bf16[768,3072]{1,0:T(8,128)(2,1)}) %all-gather.23.cloned.1.call-update) | async-done | bytes 4718608 | tf_op jit(solution)/shard_map/all_gather | solution.py:74
  551.7 64.4 %all-gather.25.cloned.1.call-done = bf16[3072,768]{1,0:T(8,128)(2,1)} async-done(((bf16[1536,768]{1,0:T(8,128)(2,1)}), bf16[3072,768]{1,0:T(8,128)(2,1)}) %all-gather.25.cloned.1.call-update) | async-done | bytes 4718608 | tf_op jit(solution)/shard_map/all_gather | solution.py:76
  628.1 134.5 %while.35 = (s32[]{:T(128)}, f32[128,12,64]{0,2,1:T(8,128)}, f32[16,512,1536]{2,1,0:T(8,128)}, s32[16]{0:T(128)S(1)}, s32[]{:T(128)}, /*index=5*/bf16[16,512,12,...) while((s32[]{:T(128)}, f32[128,12,64]{0,2,1:T(8,128)}, ...), condition=%wide.region_16.17_spmd.clone, body=%wide.region_13.16_spmd.clone.sunk | while | flops 514491008 | bytes 40333600 | solution.py:264
  629.3 10.1 conditional.7
  775.8 501.6 %reduce-scatter.6.cloned.1.call-done = f32[128,1536]{1,0:T(8,128)} async-done(((f32[8192,1536]{1,0:T(8,128)}), f32[128,1536]{1,0:T(8,128)}) %reduce-scatter.6.cloned.1.call-update) | async-done | bytes 786448 | tf_op jit(solution)/shard_map/reduce_scatter | solution.py:267
  1297.0 7.7 reduce-scatter.10.cloned.1.call-done
  1304.7 66.4 %reduce-scatter.12.cloned.1.call-done = bf16[384,3072]{1,0:T(8,128)(2,1)} async-done(((bf16[768,3072]{1,0:T(8,128)(2,1)}), bf16[384,3072]{1,0:T(8,128)(2,1)}) %reduce-scatter.12.cloned.1.call-update) | async-done | bytes 2359312 | tf_op jit(solution)/shard_map/reduce_scatter | solution.py:315
  1371.1 66.4 %reduce-scatter.14.cloned.1.call-done = bf16[1536,768]{1,0:T(8,128)(2,1)} async-done(((bf16[3072,768]{1,0:T(8,128)(2,1)}), bf16[1536,768]{1,0:T(8,128)(2,1)}) %reduce-scatter.14.cloned.1.call-update) | async-done | bytes 2359312 | tf_op jit(solution)/shard_map/reduce_scatter | solution.py:321
  1442.6 8.4 all-reduce.10
  1451.5 40.0 %reduce-scatter.8.cloned.1.call-done = bf16[384,2304]{1,0:T(8,128)(2,1)} async-done(((bf16[768,2304]{1,0:T(8,128)(2,1)}), bf16[384,2304]{1,0:T(8,128)(2,1)}) %reduce-scatter.8.cloned.1.call-update) | async-done | bytes 1769488 | tf_op jit(solution)/shard_map/reduce_scatter | solution.py:294
  1491.5 329.9 %all-reduce.12 = (f32[384]{0:T(512)}, f32[384]{0:T(512)}, f32[384,2304]{1,0:T(8,128)}, f32[384]{0:T(512)}, f32[384]{0:T(512)}, /*index=5*/f32[384,768]{1,0:T(8,1...) all-reduce(f32[384]{0:T(512)S(1)} %get-tuple-element.682, ...), channel_id=1, replica_groups=mesh['ctx'=64,'fsdp'=2] {'ctx'}, use_global_device_ids=true, to_apply=%region_22.23 | all-reduce | flops 3543552 | bytes 21270528 | tf_op jit(solution)/shard_map/psum | solution.py:328
  (404 shorter events, 259.1 us)
Async XLA Ops:
  7.2 58.5 %all-gather.17.cloned.1.call-start = ((), (), s32[]{:S(2)}) async-start(), calls=%async_computation.5 | async-start | bytes 5308416 | tf_op jit(solution)/shard_map/all_gather | solution.py:67
  7.9 178.9 %all-gather.27.cloned.1.call-start = ((), (), s32[]{:S(2)}) async-start(), calls=%async_computation.10 | async-start | bytes 12779520 | tf_op jit(solution)/shard_map/all_gather | solution.py:215
  69.3 237.1 %all-gather.29.cloned.1.call-start = ((), (), s32[]{:S(2)}) async-start(), calls=%async_computation.11 | async-start | bytes 12779520 | tf_op jit(solution)/shard_map/all_gather | solution.py:216
  81.9 369.7 %all-gather.19.cloned.1.call-start = ((), (), s32[]{:S(2)}) async-start(), calls=%async_computation.6 | async-start | bytes 25559040 | tf_op jit(solution)/shard_map/all_gather | solution.py:114
  83.8 423.1 %all-gather.21.cloned.1.call-start = ((), (), s32[]{:S(2)}) async-start(), calls=%async_computation.7 | async-start | bytes 1769472 | tf_op jit(solution)/shard_map/all_gather | solution.py:70
  84.4 464.0 %all-gather.23.cloned.1.call-start = ((), (), s32[]{:S(2)}) async-start(), calls=%async_computation.8 | async-start | bytes 7077888 | tf_op jit(solution)/shard_map/all_gather | solution.py:74
  85.0 531.1 %all-gather.25.cloned.1.call-start = ((), (), s32[]{:S(2)}) async-start(), calls=%async_computation.9 | async-start | bytes 7077888 | tf_op jit(solution)/shard_map/all_gather | solution.py:76
  85.7 1191.7 %reduce-scatter.6.cloned.1.call-start = ((), (), s32[]{:S(2)}) async-start(), calls=%async_computation.12 | async-start | bytes 51118080 | tf_op jit(solution)/shard_map/reduce_scatter | solution.py:267
  103.5 444.9 %copy-start.24 = (f32[768]{0:T(1024)}, f32[768]{0:T(1024)S(1)}, u32[]{:S(2)}) copy-start(f32[768]{0:T(1024)S(1)} %reshape.258) | copy-start | bytes 9220
  109.4 439.0 %copy-start.21 = (f32[768]{0:T(1024)}, f32[768]{0:T(1024)S(1)}, u32[]{:S(2)}) copy-start(f32[768]{0:T(1024)S(1)} %reshape.257) | copy-start | bytes 9220
  506.9 119.3 %copy-start.11 = (bf16[128,12,64]{0,2,1:T(8,128)(2,1)}, bf16[128,12,64]{0,2,1:T(8,128)(2,1)S(1)}, u32[]{:S(2)}) copy-start(bf16[128,12,64]{0,2,1:T(8,128)(2,1)S(1)} %divide_convert_fusion) | copy-start | bytes 589828
  508.7 115.2 %copy-start.1 = (f32[128,768]{1,0:T(8,128)}, f32[128,768]{1,0:T(8,128)S(1)}, u32[]{:S(2)}) copy-start(f32[128,768]{1,0:T(8,128)S(1)} %get-tuple-element.670) | copy-start | bytes 1179652
  762.6 542.1 %reduce-scatter.10.cloned.1.call-start = ((), (), s32[]{:S(2)}) async-start(), calls=%async_computation.14 | async-start | bytes 1769472 | tf_op jit(solution)/shard_map/reduce_scatter | solution.py:303
  765.2 605.9 %reduce-scatter.12.cloned.1.call-start = ((), (), s32[]{:S(2)}) async-start(), calls=%async_computation.15 | async-start | bytes 7077888 | tf_op jit(solution)/shard_map/reduce_scatter | solution.py:315
  769.1 668.4 %reduce-scatter.14.cloned.1.call-start = ((), (), s32[]{:S(2)}) async-start(), calls=%async_computation.16 | async-start | bytes 7077888 | tf_op jit(solution)/shard_map/reduce_scatter | solution.py:321
  774.3 504.3 %copy-start.20 = (f32[768]{0:T(1024)S(1)}, f32[768]{0:T(1024)}, u32[]{:S(2)}) copy-start(f32[768]{0:T(1024)} %copy-done.19) | copy-start | bytes 9220
  774.3 504.3 %copy-start.27 = (f32[768]{0:T(1024)S(1)}, f32[768]{0:T(1024)}, u32[]{:S(2)}) copy-start(f32[768]{0:T(1024)} %copy-done.26) | copy-start | bytes 9220
  774.3 504.3 %copy-start.32 = (f32[128]{0:T(128)S(1)}, f32[128]{0:T(128)}, u32[]{:S(2)}) copy-start(f32[128]{0:T(128)} %copy-done.31) | copy-start | bytes 1540
  774.3 717.2 %reduce-scatter.8.cloned.1.call-start = ((), (), s32[]{:S(2)}) async-start(), calls=%async_computation.13 | async-start | bytes 5308416 | tf_op jit(solution)/shard_map/reduce_scatter | solution.py:294
  775.8 506.5 %copy-start.17 = (bf16[128,768]{1,0:T(8,128)(2,1)}, bf16[128,768]{1,0:T(8,128)(2,1)S(1)}, u32[]{:S(2)}) copy-start(bf16[128,768]{1,0:T(8,128)(2,1)S(1)} %copy.84) | copy-start | bytes 589828
  1292.8 144.7 %copy-start.15 = (f32[128,1536]{1,0:T(8,128)S(1)}, f32[128,1536]{1,0:T(8,128)}, u32[]{:S(2)}) copy-start(f32[128,1536]{1,0:T(8,128)} %reduce-scatter.6.cloned.1.call-done) | copy-start | bytes 2359300
  1297.0 144.3 %copy-start.54 = (f32[128]{0:T(128)S(1)}, f32[128]{0:T(128)}, u32[]{:S(2)}) copy-start(f32[128]{0:T(128)} %copy-done.53) | copy-start | bytes 1540
  1297.0 144.3 %copy-start.37 = (f32[128]{0:T(128)S(1)}, f32[128]{0:T(128)}, u32[]{:S(2)}) copy-start(f32[128]{0:T(128)} %copy-done.36) | copy-start | bytes 1540
  1297.0 144.6 %copy-start.45 = (f32[128]{0:T(128)S(1)}, f32[128]{0:T(128)}, u32[]{:S(2)}) copy-start(f32[128]{0:T(128)} %copy-done.43) | copy-start | bytes 1540
  (46 other events, 844.3 us)
Sparse Core Ops, SparseCore 0:
  9.7 56.0 all-gather.16
  69.4 117.4 all-gather.26
  189.2 117.0 all-gather.28
  308.5 143.1 all-gather.18
  453.1 27.6 all-gather.20
  482.3 66.0 all-gather.22
  550.0 66.0 all-gather.24
  762.7 514.6 reduce-scatter.5
  1280.4 24.3 reduce-scatter.9
  1307.7 63.3 reduce-scatter.11
  1374.1 63.3 reduce-scatter.13
  1440.4 51.0 reduce-scatter.7
